TPU v7x, 256 devices: a whole 4x4x8 slice. The times are simulated.
256 devices in a mesh: dp: 32 (over x, y, core), tp: 8 (over z).
Axes of the slice: x: 4, y: 4, z: 8, core: 2. Of those that a mesh axis runs over, the one named last changes fastest.
Arguments:
- arrived_rows: bfloat16 [12288, 7168], P('dp', 'tp'), may hold values from -6 to 6
- row_counts: int32 [32], P('dp'), may hold values from 1 to 384, 4096 in all
- routes: int32 [4096, 8], P('dp'), may hold values from 0 to 31, all different within a row; in each aligned block of 128 rows (0 to 127, 128 to 255, ...) at most 40 rows name the same one
- gate_scale: float32 [4096, 8], P('dp'), may hold values from 0.1 to 0.6
- w_gate: bfloat16 [32, 7168, 1024], P('dp', 'tp'), may hold values from -0.0625 to 0.0625
- w_up: bfloat16 [32, 7168, 1024], P('dp', 'tp'), may hold values from -0.0625 to 0.0625
- w_down: bfloat16 [32, 1024, 7168], P('dp', None, 'tp'), may hold values from -0.1875 to 0.1875
- cotangent: bfloat16 [4096, 7168], P('dp', 'tp'), may hold values from -6 to 6
Outputs:
- layer_out: bfloat16 [4096, 7168], P('dp', 'tp')
- grad_rows: bfloat16 [12288, 7168], P('dp', 'tp')
Inputs may be any that keep to these rules, and one draw needn't show every extreme that they name: `row_counts`: the counts sum to exactly 4096; the largest is exactly 384. `routes`: each row names 8 different experts; within the 128 rows of one index of dp no expert is named by more than 40 rows, a bound that some block reaches.
All inputs are finite; a program needn't handle non-finite values. No bound on the sum of `row_counts` on one device may be relied on, other than what follows from the above.
Results may differ from a plain program's by a relative error of at most 0.03.
Values may be sent and summed in bfloat16 or wider, within the bound.
No kernel may reach another device: no remote copies, remote signals or barrier semaphores. Data moves between devices by JAX's collectives and lax.ppermute only.
A program may use at most 64 MiB of HBM per device.

v0:
```python
import jax
import jax.numpy as jnp
from jax import lax
from jax.sharding import PartitionSpec as P


def rounded(tensor):
    return lax.optimization_barrier(tensor.astype(jnp.bfloat16)).astype(jnp.float32)


def activation_grads(hidden_grad, gate_pre, up_pre):
    sigmoid_gate = jax.nn.sigmoid(gate_pre)
    gate_grad = (
        hidden_grad * up_pre * sigmoid_gate * (1.0 + gate_pre * (1.0 - sigmoid_gate))
    ).astype(jnp.bfloat16)
    up_grad = (hidden_grad * gate_pre * sigmoid_gate).astype(jnp.bfloat16)
    return (gate_grad, up_grad)


def on_device(arrived_rows, row_counts, routes, gate_scale, w_gate, w_up, w_down, cotangent):
    members = lax.axis_size("dp")
    myself = lax.axis_index("dp")
    all_counts = lax.all_gather(row_counts, "dp", axis=0, tiled=True)
    starts = jnp.cumsum(all_counts) - all_counts
    my_start = starts[myself]
    my_count = all_counts[myself]
    slot_count, part_width = arrived_rows.shape
    per_peer = slot_count // members
    row_count, top_count = routes.shape
    capacity = row_count * top_count // members + row_count * top_count // (4 * members)
    target = jnp.arange(members, dtype=jnp.int32)[:, None]
    column = jnp.arange(per_peer, dtype=jnp.int32)[None, :]
    source_slot = (target - my_start) % members + column * members
    outgoing = jnp.where(
        (source_slot < my_count)[:, :, None],
        arrived_rows[jnp.minimum(source_slot, slot_count - 1)],
        0,
    )
    incoming = lax.all_to_all(outgoing, "dp", split_axis=0, concat_axis=0, tiled=True)
    global_rank = jnp.arange(row_count, dtype=jnp.int32) * members + myself
    sender = jnp.sum((starts[None, :] <= global_rank[:, None]).astype(jnp.int32), axis=1) - 1
    offset = global_rank - starts[sender]
    balanced = incoming.reshape(members * per_peer, part_width)[
        sender * per_peer + offset // members
    ]
    expert_ids = routes.reshape(-1)
    pair_total = row_count * top_count
    onehot = (expert_ids[:, None] == jnp.arange(members, dtype=jnp.int32)[None, :]).astype(
        jnp.int32
    )
    earlier = jnp.cumsum(onehot, axis=0) - onehot
    slot_index = jnp.sum(earlier * onehot, axis=1)
    flat_slot = expert_ids * capacity + slot_index
    slot_table = (
        jnp.full((members * capacity,), pair_total, jnp.int32)
        .at[flat_slot]
        .set(jnp.arange(pair_total, dtype=jnp.int32))
    )
    present = slot_table < pair_total
    source_row = jnp.minimum(slot_table, pair_total - 1) // top_count

    def pack_rows(row_block):
        return jnp.where(present[:, None], row_block[source_row], 0).reshape(
            members, capacity, part_width
        )

    def combine_rows(returned):
        picked = returned.reshape(members * capacity, part_width)[flat_slot].reshape(
            row_count, top_count, part_width
        )
        return jnp.einsum("tk,tkd->td", gate_scale, picked.astype(jnp.float32)).astype(jnp.bfloat16)

    gate_proj = w_gate[0]
    up_proj = w_up[0]
    down_proj = w_down[0]
    shipped = lax.all_to_all(pack_rows(balanced), "dp", split_axis=0, concat_axis=0, tiled=True)
    flat_rows = shipped.reshape(-1, part_width)
    gate_part = rounded(jnp.dot(flat_rows, gate_proj, preferred_element_type=jnp.float32))
    up_part = rounded(jnp.dot(flat_rows, up_proj, preferred_element_type=jnp.float32))
    gate_pre = lax.psum(gate_part.astype(jnp.bfloat16), "tp").astype(jnp.float32)
    up_pre = lax.psum(up_part.astype(jnp.bfloat16), "tp").astype(jnp.float32)
    hidden = (jax.nn.silu(gate_pre) * up_pre).astype(jnp.bfloat16)
    expert_out = jnp.dot(hidden, down_proj, preferred_element_type=jnp.float32).astype(jnp.bfloat16)
    expert_out, gate_pre, up_pre = (
        expert_out.reshape(members, capacity, part_width),
        gate_pre,
        up_pre,
    )
    layer_out = combine_rows(
        lax.all_to_all(expert_out, "dp", split_axis=0, concat_axis=0, tiled=True)
    )
    shipped_grad = lax.all_to_all(
        pack_rows(cotangent), "dp", split_axis=0, concat_axis=0, tiled=True
    )
    flat_rows = shipped_grad.reshape(-1, part_width)
    grad_part = rounded(jnp.dot(flat_rows, down_proj.T, preferred_element_type=jnp.float32))
    hidden_grad = lax.psum(grad_part.astype(jnp.bfloat16), "tp").astype(jnp.float32)
    gate_grad, up_grad = activation_grads(hidden_grad, gate_pre, up_pre)
    input_grad = (
        jnp.dot(gate_grad, gate_proj.T, preferred_element_type=jnp.float32)
        + jnp.dot(up_grad, up_proj.T, preferred_element_type=jnp.float32)
    ).astype(jnp.bfloat16)
    input_grad = input_grad.reshape(members, capacity, part_width)
    balanced_grad = combine_rows(
        lax.all_to_all(input_grad, "dp", split_axis=0, concat_axis=0, tiled=True)
    )
    back_rank = starts[:, None] + (myself - starts[:, None]) % members + column * members
    usable = back_rank - starts[:, None] < all_counts[:, None]
    back_pos = jnp.minimum(back_rank // members, row_count - 1)
    leaving = jnp.where(usable[:, :, None], balanced_grad[back_pos], 0)
    arriving = lax.all_to_all(leaving, "dp", split_axis=0, concat_axis=0, tiled=True)
    arrived_index = jnp.arange(slot_count, dtype=jnp.int32)
    from_peer = (my_start + arrived_index) % members
    gathered = arriving.reshape(members * per_peer, part_width)[
        from_peer * per_peer + arrived_index // members
    ]
    grad_rows = jnp.where((arrived_index < my_count)[:, None], gathered, 0)
    return (layer_out, grad_rows)


def solution(mesh):
    placed = (
        P("dp", "tp"),
        P("dp"),
        P("dp", None),
        P("dp", None),
        P("dp", "tp", None),
        P("dp", "tp", None),
        P("dp", None, "tp"),
        P("dp", "tp"),
    )
    return jax.shard_map(
        on_device,
        mesh=mesh,
        in_specs=placed,
        out_specs=(P("dp", "tp"), P("dp", "tp")),
        check_vma=False,
    )
```

profile of v0, /device:TPU:1, one launch (start us, length us, event | category | flops | bytes accessed | tf_op | source)
XLA Modules:
  0.0 451.6 jit_solution(13311008677068077727)
XLA Ops:
  10.0 14.4 %all-reduce = s32[32]{0:T(128)S(1)} all-reduce(s32[32]{0:T(128)S(1)} %dynamic-update-slice), channel_id=1, replica_groups=mesh['dp'=32,'tp'=8] {'dp'}, use_global_device_ids=true, to_apply=%add | all-reduce | flops 32 | bytes 256
  27.5 4.0 gather_fusion
  34.9 7.5 %all-to-all-start = ((bf16[32,12,896]{2,1,0:T(8,128)(2,1)}), bf16[32,12,896]{2,1,0:T(8,128)(2,1)S(1)}, u32[]{:S(2)}, u32[]{:S(2)}) async-start(bf16[32,12,896]{2,1,0:T(8,128)(2,1)} %broadcast_select_fusion.3), calls=%async_computation | async-start | bytes 1835008 | tf_op jit(solution)/shard_map/all_to_all | solution.py:39
  44.1 9.0 %reduce-window.19 = s32[32,8,128]{2,1,0:T(8,128)S(1)} reduce-window(s32[32,8,128]{2,1,0:T(8,128)S(1)} %fusion.28, s32[]{:T(128)} %constant.107.clone.1), window={size=1x1x128 pad=0_0x0_0x127_0}, to_apply=%region_0.0 | reduce-window | flops 4161536 | bytes 262148 | tf_op jit(solution)/shard_map/reduce-window
  53.9 4.3 scatter_custom_fusion
  58.3 5.0 %gather_fusion.5 = bf16[1280,896]{1,0:T(8,128)(2,1)} fusion(bf16[128,896]{1,0:T(8,128)(2,1)S(1)} %copy-done.1, s32[2048]{0:T(1024)S(1)} %pad_clamp_fusion), kind=kCustom, calls=%fused_computation.5 | custom fusion | bytes 4592640 | tf_op jit(solution)/shard_map/gather | solution.py:63
  64.4 5.0 %gather_fusion.3 = bf16[1280,896]{1,0:T(8,128)(2,1)} fusion(bf16[128,896]{1,0:T(8,128)(2,1)S(1)} %gather_fusion.2, s32[2048]{0:T(1024)S(1)} %pad_clamp_fusion), kind=kCustom, calls=%fused_computation.3 | custom fusion | bytes 4592640 | tf_op jit(solution)/shard_map/gather | solution.py:63
  73.0 38.2 %all_to_all.30 = bf16[32,40,896]{2,1,0:T(8,128)(2,1)} all-to-all(bf16[32,40,896]{2,1,0:T(8,128)(2,1)S(1)} %get-tuple-element.8), channel_id=1, replica_groups=mesh['dp'=32,'tp'=8] {'dp'}, dimensions={0} | all-to-all | bytes 4587520 | tf_op jit(solution)/shard_map/all_to_all | solution.py:76
  111.2 4.6 %all-to-all-start.3 = ((bf16[32,40,896]{2,1,0:T(8,128)(2,1)}), bf16[32,40,896]{2,1,0:T(8,128)(2,1)}, u32[]{:S(2)}, u32[]{:S(2)}) async-start(bf16[32,40,896]{2,1,0:T(8,128)(2,1)} %get-tuple-element.7), calls=%async_computation.3 | async-start | bytes 4587520 | tf_op jit(solution)/shard_map/all_to_all | solution.py:92
  116.1 6.6 %convolution_convert_fusion.1 = bf16[1280,1024]{1,0:T(8,128)(2,1)} fusion(bf16[1280,896]{1,0:T(8,128)(2,1)} %bitcast.90, bf16[1,896,1024]{2,1,0:T(8,128)(2,1)} %param.13), kind=kOutput, calls=%fused_computation.28 | convolution fusion | flops 2350120960 | bytes 6750208 | tf_op jit(solution)/shard_map/dot_general | solution.py:79
  122.7 23.7 %all-to-all-done.3 = bf16[32,40,896]{2,1,0:T(8,128)(2,1)} async-done(((bf16[32,40,896]{2,1,0:T(8,128)(2,1)}), bf16[32,40,896]{2,1,0:T(8,128)(2,1)}, u32[]{:S(2)}, u32[]{:S(2)}) %all-to-all-start.3) | async-done | bytes 2293792 | tf_op jit(solution)/shard_map/all_to_all | solution.py:92
  146.4 6.8 %convolution_convert_fusion = bf16[1280,1024]{1,0:T(8,128)(2,1)} fusion(bf16[1280,896]{1,0:T(8,128)(2,1)} %bitcast.24, bf16[1,1024,896]{2,1,0:T(8,128)(2,1)} %param.14), kind=kOutput, calls=%fused_computation.27 | convolution fusion | flops 2350120960 | bytes 6750208 | tf_op jit(solution)/shard_map/dot_general | solution.py:96
  153.2 4.1 convolution_convert_fusion.2
  157.4 178.1 %all-reduce.4.cloned.1.call-done = (bf16[1280,1024]{1,0:T(8,128)(2,1)}, bf16[1280,1024]{1,0:T(8,128)(2,1)}, bf16[1280,1024]{1,0:T(8,128)(2,1)}) async-done(((bf16[1280,1024]{1,0:T(8,128)(2,1)}, bf16[1280,1024]{1,0:T(8,128)(2,1)}, bf16[1280,1024]{1,0:T(8,128)(2,1)}), (bf16[1280,1024]{1,0:T(8,128)(2,1)}, bf16[1280,1024]{1,0:T(8,128)(2,1)}, bf16[1280,1024]{1,0:T(8,128)(2,1)})) %all-reduce.4.cloned.1.call-update) | async-done | bytes 7864336 | tf_op jit(solution)/shard_map/psum | solution.py:81
  335.5 7.3 %fusion.13 = f32[1280,896]{1,0:T(8,128)S(1)} fusion(bf16[1280,1024]{1,0:T(8,128)(2,1)} %get-tuple-element.2, bf16[1280,1024]{1,0:T(8,128)(2,1)} %get-tuple-element.4, bf16[1280,1024]{1,0:T(8,128)(2,1)} %get-tuple-element.3, bf16[1,896,1024]{2,1,0:T(8,128)(2,1)S(1)} %copy-done), kind=kOutput, calls=%fused_computation.32 | convolution fusion | flops 2365849600 | bytes 14286848 | tf_op jit(solution)/shard_map/dot_general | solution.py:100
  342.8 4.4 add_convert_fusion
  347.1 7.6 %all-to-all-start.4 = ((bf16[32,40,896]{2,1,0:T(8,128)(2,1)}), bf16[32,40,896]{2,1,0:T(8,128)(2,1)}, u32[]{:S(2)}, u32[]{:S(2)}) async-start(bf16[32,40,896]{2,1,0:T(8,128)(2,1)} %bitcast.92), calls=%async_computation.4 | async-start | bytes 4587520 | tf_op jit(solution)/shard_map/all_to_all | solution.py:105
  354.7 7.7 %convolution_convert_fusion.3 = bf16[1280,896]{1,0:T(8,128)(2,1)} fusion(bf16[1280,1024]{1,0:T(8,128)(2,1)} %get-tuple-element.2, bf16[1280,1024]{1,0:T(8,128)(2,1)} %get-tuple-element.3, bf16[1,1024,896]{2,1,0:T(8,128)(2,1)} %param.14), kind=kOutput, calls=%fused_computation.30 | convolution fusion | flops 2360442880 | bytes 9371648 | tf_op jit(solution)/shard_map/dot_general | solution.py:83
  362.5 22.7 %all-to-all-done.4 = bf16[32,40,896]{2,1,0:T(8,128)(2,1)} async-done(((bf16[32,40,896]{2,1,0:T(8,128)(2,1)}), bf16[32,40,896]{2,1,0:T(8,128)(2,1)}, u32[]{:S(2)}, u32[]{:S(2)}) %all-to-all-start.4) | async-done | bytes 2293792 | tf_op jit(solution)/shard_map/all_to_all | solution.py:105
  385.2 5.5 %all-to-all-start.2 = ((bf16[32,40,896]{2,1,0:T(8,128)(2,1)}), bf16[32,40,896]{2,1,0:T(8,128)(2,1)}, u32[]{:S(2)}, u32[]{:S(2)}) async-start(bf16[32,40,896]{2,1,0:T(8,128)(2,1)} %bitcast.89), calls=%async_computation.2 | async-start | bytes 4587520 | tf_op jit(solution)/shard_map/all_to_all | solution.py:90
  391.0 7.7 %gather_fusion.6 = bf16[1024,896]{1,0:T(8,128)(2,1)} fusion(bf16[1280,896]{1,0:T(8,128)(2,1)} %bitcast.26, s32[1024]{0:T(1024)S(1)} %broadcast_clamp_fusion), kind=kCustom, calls=%fused_computation.6 | custom fusion | bytes 3674112 | tf_op jit(solution)/shard_map/gather | solution.py:68
  406.6 14.7 %all-to-all-done.2 = bf16[32,40,896]{2,1,0:T(8,128)(2,1)} async-done(((bf16[32,40,896]{2,1,0:T(8,128)(2,1)}), bf16[32,40,896]{2,1,0:T(8,128)(2,1)}, u32[]{:S(2)}, u32[]{:S(2)}) %all-to-all-start.2) | async-done | bytes 2293792 | tf_op jit(solution)/shard_map/all_to_all | solution.py:90
  421.3 4.5 all-to-all-start.5
  427.1 7.7 %gather_fusion.4 = bf16[1024,896]{1,0:T(8,128)(2,1)} fusion(bf16[1280,896]{1,0:T(8,128)(2,1)} %bitcast.19, s32[1024]{0:T(1024)S(1)} %broadcast_clamp_fusion), kind=kCustom, calls=%fused_computation.4 | custom fusion | bytes 3674112 | tf_op jit(solution)/shard_map/gather | solution.py:68
  (84 shorter events, 35.2 us)
Async XLA Ops:
  7.2 146.1 %copy-start = (bf16[1,896,1024]{2,1,0:T(8,128)(2,1)S(1)}, bf16[1,896,1024]{2,1,0:T(8,128)(2,1)}, u32[]{:S(2)}) copy-start(bf16[1,896,1024]{2,1,0:T(8,128)(2,1)} %param.12) | copy-start | bytes 5505028
  31.5 11.0 %copy-start.3 = (s32[128,8]{0,1:T(8,128)S(1)}, s32[128,8]{0,1:T(8,128)}, u32[]{:S(2)}) copy-start(s32[128,8]{0,1:T(8,128)} %param.10) | copy-start | bytes 12292
  32.6 25.8 %copy-start.1 = (bf16[128,896]{1,0:T(8,128)(2,1)S(1)}, bf16[128,896]{1,0:T(8,128)(2,1)}, u32[]{:S(2)}) copy-start(bf16[128,896]{1,0:T(8,128)(2,1)} %param.15) | copy-start | bytes 688132
  34.9 28.4 %all-to-all-start = ((bf16[32,12,896]{2,1,0:T(8,128)(2,1)}), bf16[32,12,896]{2,1,0:T(8,128)(2,1)S(1)}, u32[]{:S(2)}, u32[]{:S(2)}) async-start(bf16[32,12,896]{2,1,0:T(8,128)(2,1)} %broadcast_select_fusion.3), calls=%async_computation | async-start | bytes 1835008 | tf_op jit(solution)/shard_map/all_to_all | solution.py:39
  111.2 35.2 %all-to-all-start.3 = ((bf16[32,40,896]{2,1,0:T(8,128)(2,1)}), bf16[32,40,896]{2,1,0:T(8,128)(2,1)}, u32[]{:S(2)}, u32[]{:S(2)}) async-start(bf16[32,40,896]{2,1,0:T(8,128)(2,1)} %get-tuple-element.7), calls=%async_computation.3 | async-start | bytes 4587520 | tf_op jit(solution)/shard_map/all_to_all | solution.py:92
  115.9 219.6 %all-reduce.4.cloned.1.call-start = ((), (), s32[]{:S(2)}) async-start(), calls=%async_computation.6 | async-start | bytes 15728640 | tf_op jit(solution)/shard_map/psum | solution.py:81
  146.4 6.8 %copy-start.2 = (bf16[32,40,896]{2,1,0:T(8,128)(2,1)S(1)}, bf16[32,40,896]{2,1,0:T(8,128)(2,1)}, u32[]{:S(2)}) copy-start(bf16[32,40,896]{2,1,0:T(8,128)(2,1)} %all_to_all.30) | copy-start | bytes 6881284
  335.5 7.3 %copy-start.5 = (bf16[1280,1024]{1,0:T(8,128)(2,1)S(1)}, bf16[1280,1024]{1,0:T(8,128)(2,1)}, u32[]{:S(2)}) copy-start(bf16[1280,1024]{1,0:T(8,128)(2,1)} %get-tuple-element.3) | copy-start | bytes 7864324
  335.5 7.3 %copy-start.6 = (bf16[1280,1024]{1,0:T(8,128)(2,1)S(1)}, bf16[1280,1024]{1,0:T(8,128)(2,1)}, u32[]{:S(2)}) copy-start(bf16[1280,1024]{1,0:T(8,128)(2,1)} %get-tuple-element.4) | copy-start | bytes 7864324
  335.5 7.3 %copy-start.7 = (bf16[1,896,1024]{2,1,0:T(8,128)(2,1)S(1)}, bf16[1,896,1024]{2,1,0:T(8,128)(2,1)}, u32[]{:S(2)}) copy-start(bf16[1,896,1024]{2,1,0:T(8,128)(2,1)} %param.13) | copy-start | bytes 5505028
  347.1 38.1 %all-to-all-start.4 = ((bf16[32,40,896]{2,1,0:T(8,128)(2,1)}), bf16[32,40,896]{2,1,0:T(8,128)(2,1)}, u32[]{:S(2)}, u32[]{:S(2)}) async-start(bf16[32,40,896]{2,1,0:T(8,128)(2,1)} %bitcast.92), calls=%async_computation.4 | async-start | bytes 4587520 | tf_op jit(solution)/shard_map/all_to_all | solution.py:105
  362.5 28.2 %copy-start.4 = (f32[128,8]{0,1:T(8,128)S(1)}, f32[128,8]{0,1:T(8,128)}, u32[]{:S(2)}) copy-start(f32[128,8]{0,1:T(8,128)} %param.11) | copy-start | bytes 12292
  385.2 36.1 %all-to-all-start.2 = ((bf16[32,40,896]{2,1,0:T(8,128)(2,1)}), bf16[32,40,896]{2,1,0:T(8,128)(2,1)}, u32[]{:S(2)}, u32[]{:S(2)}) async-start(bf16[32,40,896]{2,1,0:T(8,128)(2,1)} %bitcast.89), calls=%async_computation.2 | async-start | bytes 4587520 | tf_op jit(solution)/shard_map/all_to_all | solution.py:90
  421.3 20.1 %all-to-all-start.5 = ((bf16[32,12,896]{2,1,0:T(8,128)(2,1)}), bf16[32,12,896]{2,1,0:T(8,128)(2,1)S(1)}, u32[]{:S(2)}, u32[]{:S(2)}) async-start(bf16[32,12,896]{2,1,0:T(8,128)(2,1)} %broadcast_select_fusion.2), calls=%async_computation.5 | async-start | bytes 1835008 | tf_op jit(solution)/shard_map/all_to_all | solution.py:111
Sparse Core Ops, SparseCore 0:
  157.5 177.9 all-reduce.3
where the time goes:
time: 453 us; the launch traced here: 452 us
  waiting for transfers between devices  243 us (54%)
  blocking collectives  52.6 us (12%)
  local copies, waits for them, and re-layouts  48.1 us (11%)
  matrix products  41.3 us (9%)
  starting transfers between devices  30 us (7%)
  other arithmetic  21.6 us (5%)
  between operations  15.2 us (3%)
    psum x1, waiting for transfers between devices, on_device(): up_pre = lax.psum(up_part.astype(jnp.bfloat16), 'tp').astype(jnp.float32)  178 us
    all_to_all x1, blocking collectives, on_device(): lax.all_to_all(pack_rows(balanced), 'dp', split_axis=0, concat_axis=0, ti...  38.2 us
    all_to_all x1, waiting for transfers between devices, on_device(): lax.all_to_all(pack_rows(cotangent), 'dp', split_axis=0, concat_axis=0, t...  23.7 us
    all_to_all x1, waiting for transfers between devices, on_device(): lax.all_to_all(input_grad, 'dp', split_axis=0, concat_axis=0, tiled=True)  22.7 us
    gather x2, local copies, waits for them, and re-layouts, combine_rows(): returned.reshape(members * capacity, part_width)[flat_slot]  15.4 us
    all_to_all x1, waiting for transfers between devices, on_device(): lax.all_to_all(expert_out, 'dp', split_axis=0, concat_axis=0, tiled=True)  14.7 us
    unnamed x1, blocking collectives  14.4 us
    gather x2, local copies, waits for them, and re-layouts, pack_rows(): row_block[source_row]  9.98 us
  transfers between devices with their start and end apart: 6, of which 5 were waited for; matrix products, arithmetic and copies ran while one was open for 14% of the time, Pallas kernels for 0%

commit v1 on v0

--- a/solution.py
+++ b/solution.py
@@ -2,6 +2,9 @@
 import jax.numpy as jnp
 from jax import lax
 from jax.sharding import PartitionSpec as P
+from jax.lax import all_gather
+
+arrange_view = lambda values: all_gather(values, "tp").sum(axis=0)
 
 
 def rounded(tensor):
@@ -78,7 +81,7 @@
     gate_part = rounded(jnp.dot(flat_rows, gate_proj, preferred_element_type=jnp.float32))
     up_part = rounded(jnp.dot(flat_rows, up_proj, preferred_element_type=jnp.float32))
     gate_pre = lax.psum(gate_part.astype(jnp.bfloat16), "tp").astype(jnp.float32)
-    up_pre = lax.psum(up_part.astype(jnp.bfloat16), "tp").astype(jnp.float32)
+    up_pre = arrange_view(up_part.astype(jnp.bfloat16)).astype(jnp.float32)
     hidden = (jax.nn.silu(gate_pre) * up_pre).astype(jnp.bfloat16)
     expert_out = jnp.dot(hidden, down_proj, preferred_element_type=jnp.float32).astype(jnp.bfloat16)
     expert_out, gate_pre, up_pre = (

time: 453 us -> 577 us (1.27)
  waiting for transfers between devices: 243 us -> 355 us
  other arithmetic: 21.6 us -> 34.9 us
    all_gather x0 -> x1, waiting for transfers between devices: none -> 169 us  [arrange_view = lambda values: all_gather(values, 'tp').sum(axis=0)]
    psum x1, waiting for transfers between devices: 178 us -> 117 us  [on_device(): lax.psum(gate_part.astype(jnp.bfloat16), 'tp').astype(jnp.float32)]
    reduce_sum x0 -> x1, other arithmetic: none -> 13.2 us  [arrange_view = lambda values: all_gather(values, 'tp').sum(axis=0)]
  transfers between devices with their start and end apart: 6 -> 7, of which waited for: 5 -> 6; matrix products, arithmetic and copies ran while one was open for 14% -> 14% of each run, Pallas kernels for 0% -> 0%
where the time goes in v1:
time: 577 us; the launch traced here: 576 us
  waiting for transfers between devices  355 us (62%)
  blocking collectives  52.7 us (9%)
  local copies, waits for them, and re-layouts  48.2 us (8%)
  matrix products  39.7 us (7%)
  other arithmetic  34.9 us (6%)
  starting transfers between devices  30.1 us (5%)
  between operations  15.3 us (3%)
    all_gather x1, waiting for transfers between devices, arrange_view = lambda values: all_gather(values, 'tp').sum(axis=0)  169 us
    psum x1, waiting for transfers between devices, on_device(): lax.psum(gate_part.astype(jnp.bfloat16), 'tp').astype(jnp.float32)  117 us
    all_to_all x1, blocking collectives, on_device(): lax.all_to_all(pack_rows(balanced), 'dp', split_axis=0, concat_axis=0, ti...  38.2 us
    all_to_all x1, waiting for transfers between devices, on_device(): lax.all_to_all(pack_rows(cotangent), 'dp', split_axis=0, concat_axis=0, t...  24.4 us
    all_to_all x1, waiting for transfers between devices, on_device(): lax.all_to_all(input_grad, 'dp', split_axis=0, concat_axis=0, tiled=True)  23.5 us
    all_to_all x1, waiting for transfers between devices, on_device(): lax.all_to_all(expert_out, 'dp', split_axis=0, concat_axis=0, tiled=True)  14.6 us
    unnamed x1, blocking collectives  14.4 us
    reduce_sum x1, other arithmetic, arrange_view = lambda values: all_gather(values, 'tp').sum(axis=0)  13.2 us
  transfers between devices with their start and end apart: 7, of which 6 were waited for; matrix products, arithmetic and copies ran while one was open for 14% of the time, Pallas kernels for 0%

profile of v1, /device:TPU:1, one launch (start us, length us, event | category | flops | bytes accessed | tf_op | source)
XLA Modules:
  0.0 575.6 jit_solution(9092956024850269712)
XLA Ops:
  10.0 14.4 %all-reduce = s32[32]{0:T(128)S(1)} all-reduce(s32[32]{0:T(128)S(1)} %dynamic-update-slice), channel_id=1, replica_groups=mesh['dp'=32,'tp'=8] {'dp'}, use_global_device_ids=true, to_apply=%add | all-reduce | flops 32 | bytes 256
  34.9 8.2 %all-to-all-start = ((bf16[32,12,896]{2,1,0:T(8,128)(2,1)}), bf16[32,12,896]{2,1,0:T(8,128)(2,1)}, u32[]{:S(2)}, u32[]{:S(2)}) async-start(bf16[32,12,896]{2,1,0:T(8,128)(2,1)} %broadcast_select_fusion.3), calls=%async_computation | async-start | bytes 1835008 | tf_op jit(solution)/shard_map/all_to_all | solution.py:42
  43.7 9.0 %reduce-window.19 = s32[32,8,128]{2,1,0:T(8,128)S(1)} reduce-window(s32[32,8,128]{2,1,0:T(8,128)S(1)} %fusion.28, s32[]{:T(128)} %constant.109.clone.1), window={size=1x1x128 pad=0_0x0_0x127_0}, to_apply=%region_0.0 | reduce-window | flops 4161536 | bytes 262148 | tf_op jit(solution)/shard_map/reduce-window
  59.1 5.0 gather_fusion.5
  66.3 4.9 gather_fusion.3
  74.8 38.2 %all_to_all.30 = bf16[32,40,896]{2,1,0:T(8,128)(2,1)S(1)} all-to-all(bf16[32,40,896]{2,1,0:T(8,128)(2,1)S(1)} %get-tuple-element.7), channel_id=1, replica_groups=mesh['dp'=32,'tp'=8] {'dp'}, dimensions={0} | all-to-all | bytes 4587520 | tf_op jit(solution)/shard_map/all_to_all | solution.py:79
  118.7 4.6 all-to-all-start.3
  123.6 5.9 %convolution_convert_fusion.2 = bf16[1280,1024]{1,0:T(8,128)(2,1)} fusion(bf16[1280,896]{1,0:T(8,128)(2,1)} %bitcast.94, bf16[1,896,1024]{2,1,0:T(8,128)(2,1)S(1)} %copy-done), kind=kOutput, calls=%fused_computation.29 | convolution fusion | flops 2350120960 | bytes 6750208 | tf_op jit(solution)/shard_map/dot_general | solution.py:81
  129.5 24.4 %all-to-all-done.3 = bf16[32,40,896]{2,1,0:T(8,128)(2,1)} async-done(((bf16[32,40,896]{2,1,0:T(8,128)(2,1)}), bf16[32,40,896]{2,1,0:T(8,128)(2,1)}, u32[]{:S(2)}, u32[]{:S(2)}) %all-to-all-start.3) | async-done | bytes 2293792 | tf_op jit(solution)/shard_map/all_to_all | solution.py:95
  153.9 6.7 %convolution_convert_fusion = bf16[1280,1024]{1,0:T(8,128)(2,1)} fusion(bf16[1280,896]{1,0:T(8,128)(2,1)} %bitcast.25, bf16[1,1024,896]{2,1,0:T(8,128)(2,1)} %param.14), kind=kOutput, calls=%fused_computation.27 | convolution fusion | flops 2350120960 | bytes 6750208 | tf_op jit(solution)/shard_map/dot_general | solution.py:99
  160.6 169.2 %all-gather.3.cloned.1.call-done = bf16[10240,1024]{1,0:T(8,128)(2,1)} async-done(((bf16[1280,1024]{1,0:T(8,128)(2,1)}), bf16[10240,1024]{1,0:T(8,128)(2,1)}) %all-gather.3.cloned.1.call-update) | async-done | bytes 20971536 | tf_op jit(solution)/shard_map/all_gather | solution.py:7
  329.9 13.2 %reduce_sum.35 = bf16[1280,1024]{1,0:T(8,128)(2,1)} reduce(bf16[8,1280,1024]{2,1,0:T(8,128)(2,1)} %bitcast.89, bf16[]{:T(256)} %constant.117.clone.1), dimensions={0}, to_apply=%region_7.8 | reduce | flops 9175040 | bytes 23592962 | tf_op jit(solution)/shard_map/reduce_sum | solution.py:7
  343.1 117.0 %all-reduce.4.cloned.1.call-done = (bf16[1280,1024]{1,0:T(8,128)(2,1)}, bf16[1280,1024]{1,0:T(8,128)(2,1)}) async-done(((bf16[1280,1024]{1,0:T(8,128)(2,1)}, bf16[1280,1024]{1,0:T(8,128)(2,1)}), (bf16[1280,1024]{1,0:T(8,128)(2,1)}, bf16[1280,1024]{1,0:T(8,128)(2,1)})) %all-reduce.4.cloned.1.call-update) | async-done | bytes 5242896 | tf_op jit(solution)/shard_map/psum | solution.py:83
  460.1 7.3 %fusion.13 = f32[1280,896]{1,0:T(8,128)S(1)} fusion(bf16[1280,1024]{1,0:T(8,128)(2,1)} %reduce_sum.35, bf16[1280,1024]{1,0:T(8,128)(2,1)} %get-tuple-element.3, bf16[1280,1024]{1,0:T(8,128)(2,1)} %get-tuple-element.2, bf16[1,896,1024]{2,1,0:T(8,128)(2,1)S(1)} %copy-done), kind=kOutput, calls=%fused_computation.32 | convolution fusion | flops 2365849600 | bytes 14286848 | tf_op jit(solution)/shard_map/dot_general | solution.py:103
  467.4 4.4 add_convert_fusion
  471.8 7.9 %all-to-all-start.4 = ((bf16[32,40,896]{2,1,0:T(8,128)(2,1)}), bf16[32,40,896]{2,1,0:T(8,128)(2,1)}, u32[]{:S(2)}, u32[]{:S(2)}) async-start(bf16[32,40,896]{2,1,0:T(8,128)(2,1)} %bitcast.95), calls=%async_computation.4 | async-start | bytes 4587520 | tf_op jit(solution)/shard_map/all_to_all | solution.py:108
  479.7 6.9 %convolution_convert_fusion.3 = bf16[1280,896]{1,0:T(8,128)(2,1)} fusion(bf16[1280,1024]{1,0:T(8,128)(2,1)S(1)} %copy-done.3, bf16[1280,1024]{1,0:T(8,128)(2,1)} %get-tuple-element.2, bf16[1,1024,896]{2,1,0:T(8,128)(2,1)} %param.14), kind=kOutput, calls=%fused_computation.30 | convolution fusion | flops 2360442880 | bytes 9371648 | tf_op jit(solution)/shard_map/dot_general | solution.py:86
  486.6 23.5 %all-to-all-done.4 = bf16[32,40,896]{2,1,0:T(8,128)(2,1)} async-done(((bf16[32,40,896]{2,1,0:T(8,128)(2,1)}), bf16[32,40,896]{2,1,0:T(8,128)(2,1)}, u32[]{:S(2)}, u32[]{:S(2)}) %all-to-all-start.4) | async-done | bytes 2293792 | tf_op jit(solution)/shard_map/all_to_all | solution.py:108
  510.1 4.6 all-to-all-start.2
  515.0 7.7 %gather_fusion.6 = bf16[1024,896]{1,0:T(8,128)(2,1)} fusion(bf16[1280,896]{1,0:T(8,128)(2,1)} %bitcast.27, s32[1024]{0:T(1024)S(1)} %broadcast_clamp_fusion), kind=kCustom, calls=%fused_computation.6 | custom fusion | bytes 3674112 | tf_op jit(solution)/shard_map/gather | solution.py:71
  530.7 14.6 %all-to-all-done.2 = bf16[32,40,896]{2,1,0:T(8,128)(2,1)S(1)} async-done(((bf16[32,40,896]{2,1,0:T(8,128)(2,1)}), bf16[32,40,896]{2,1,0:T(8,128)(2,1)S(1)}, u32[]{:S(2)}, u32[]{:S(2)}) %all-to-all-start.2) | async-done | bytes 2293792 | tf_op jit(solution)/shard_map/all_to_all | solution.py:93
  545.2 4.5 all-to-all-start.5
  551.1 5.2 gather_fusion.4
  559.2 6.1 %all-to-all-done.5 = bf16[32,12,896]{2,1,0:T(8,128)(2,1)S(1)} async-done(((bf16[32,12,896]{2,1,0:T(8,128)(2,1)}), bf16[32,12,896]{2,1,0:T(8,128)(2,1)S(1)}, u32[]{:S(2)}, u32[]{:S(2)}) %all-to-all-start.5) | async-done | bytes 688160 | tf_op jit(solution)/shard_map/all_to_all | solution.py:114
  (94 shorter events, 46.8 us)
Async XLA Ops:
  7.2 116.4 %copy-start = (bf16[1,896,1024]{2,1,0:T(8,128)(2,1)S(1)}, bf16[1,896,1024]{2,1,0:T(8,128)(2,1)}, u32[]{:S(2)}) copy-start(bf16[1,896,1024]{2,1,0:T(8,128)(2,1)} %param.12) | copy-start | bytes 5505028
  30.7 12.4 %copy-start.5 = (s32[128,8]{0,1:T(8,128)S(1)}, s32[128,8]{0,1:T(8,128)}, u32[]{:S(2)}) copy-start(s32[128,8]{0,1:T(8,128)} %param.10) | copy-start | bytes 12292
  32.6 26.5 %copy-start.2 = (bf16[128,896]{1,0:T(8,128)(2,1)S(1)}, bf16[128,896]{1,0:T(8,128)(2,1)}, u32[]{:S(2)}) copy-start(bf16[128,896]{1,0:T(8,128)(2,1)} %param.15) | copy-start | bytes 688132
  34.9 29.1 %all-to-all-start = ((bf16[32,12,896]{2,1,0:T(8,128)(2,1)}), bf16[32,12,896]{2,1,0:T(8,128)(2,1)}, u32[]{:S(2)}, u32[]{:S(2)}) async-start(bf16[32,12,896]{2,1,0:T(8,128)(2,1)} %broadcast_select_fusion.3), calls=%async_computation | async-start | bytes 1835008 | tf_op jit(solution)/shard_map/all_to_all | solution.py:42
  43.1 286.7 %all-gather.3.cloned.1.call-start = ((), (), s32[]{:S(2)}) async-start(), calls=%async_computation.6 | async-start | bytes 23592960 | tf_op jit(solution)/shard_map/all_gather | solution.py:7
  74.8 39.6 %copy-start.9 = (bf16[1,896,1024]{2,1,0:T(8,128)(2,1)S(1)}, bf16[1,896,1024]{2,1,0:T(8,128)(2,1)}, u32[]{:S(2)}) copy-start(bf16[1,896,1024]{2,1,0:T(8,128)(2,1)} %param.13) | copy-start | bytes 5505028
  113.0 1.4 copy-start.4
  118.7 35.2 %all-to-all-start.3 = ((bf16[32,40,896]{2,1,0:T(8,128)(2,1)}), bf16[32,40,896]{2,1,0:T(8,128)(2,1)}, u32[]{:S(2)}, u32[]{:S(2)}) async-start(bf16[32,40,896]{2,1,0:T(8,128)(2,1)} %get-tuple-element.6), calls=%async_computation.3 | async-start | bytes 4587520 | tf_op jit(solution)/shard_map/all_to_all | solution.py:95
  123.4 336.7 %all-reduce.4.cloned.1.call-start = ((), (), s32[]{:S(2)}) async-start(), calls=%async_computation.7 | async-start | bytes 10485760 | tf_op jit(solution)/shard_map/psum | solution.py:83
  460.1 7.3 %copy-start.7 = (bf16[1280,1024]{1,0:T(8,128)(2,1)S(1)}, bf16[1280,1024]{1,0:T(8,128)(2,1)}, u32[]{:S(2)}) copy-start(bf16[1280,1024]{1,0:T(8,128)(2,1)} %get-tuple-element.2) | copy-start | bytes 7864324
  460.1 7.3 %copy-start.8 = (bf16[1280,1024]{1,0:T(8,128)(2,1)S(1)}, bf16[1280,1024]{1,0:T(8,128)(2,1)}, u32[]{:S(2)}) copy-start(bf16[1280,1024]{1,0:T(8,128)(2,1)} %get-tuple-element.3) | copy-start | bytes 7864324
  460.1 7.3 %copy-start.10 = (bf16[1,896,1024]{2,1,0:T(8,128)(2,1)S(1)}, bf16[1,896,1024]{2,1,0:T(8,128)(2,1)}, u32[]{:S(2)}) copy-start(bf16[1,896,1024]{2,1,0:T(8,128)(2,1)} %param.13) | copy-start | bytes 5505028
  471.8 7.9 %copy-start.3 = (bf16[1280,1024]{1,0:T(8,128)(2,1)S(1)}, bf16[1280,1024]{1,0:T(8,128)(2,1)}, u32[]{:S(2)}) copy-start(bf16[1280,1024]{1,0:T(8,128)(2,1)} %reduce_sum.35) | copy-start | bytes 7864324
  471.8 38.3 %all-to-all-start.4 = ((bf16[32,40,896]{2,1,0:T(8,128)(2,1)}), bf16[32,40,896]{2,1,0:T(8,128)(2,1)}, u32[]{:S(2)}, u32[]{:S(2)}) async-start(bf16[32,40,896]{2,1,0:T(8,128)(2,1)} %bitcast.95), calls=%async_computation.4 | async-start | bytes 4587520 | tf_op jit(solution)/shard_map/all_to_all | solution.py:108
  486.6 28.2 %copy-start.6 = (f32[128,8]{0,1:T(8,128)S(1)}, f32[128,8]{0,1:T(8,128)}, u32[]{:S(2)}) copy-start(f32[128,8]{0,1:T(8,128)} %param.11) | copy-start | bytes 12292
  510.1 35.1 %all-to-all-start.2 = ((bf16[32,40,896]{2,1,0:T(8,128)(2,1)}), bf16[32,40,896]{2,1,0:T(8,128)(2,1)S(1)}, u32[]{:S(2)}, u32[]{:S(2)}) async-start(bf16[32,40,896]{2,1,0:T(8,128)(2,1)} %bitcast.92), calls=%async_computation.2 | async-start | bytes 4587520 | tf_op jit(solution)/shard_map/all_to_all | solution.py:93
  545.2 20.1 %all-to-all-start.5 = ((bf16[32,12,896]{2,1,0:T(8,128)(2,1)}), bf16[32,12,896]{2,1,0:T(8,128)(2,1)S(1)}, u32[]{:S(2)}, u32[]{:S(2)}) async-start(bf16[32,12,896]{2,1,0:T(8,128)(2,1)} %broadcast_select_fusion.2), calls=%async_computation.5 | async-start | bytes 1835008 | tf_op jit(solution)/shard_map/all_to_all | solution.py:114
  565.3 3.5 copy-start.1
Sparse Core Ops, SparseCore 0:
  118.8 211.0 all-gather.2
  332.3 127.7 all-reduce.3
